TPU v7x, 256 devices: a whole 4x4x8 slice. The times are simulated.
256 devices in a mesh: pipe: 8 (over z), seq: 16 (over x, y), tp: 2 (over core).
Axes of the slice: x: 4, y: 4, z: 8, core: 2. Of those that a mesh axis runs over, the one named last changes fastest.
Arguments:
- layer_inputs: bfloat16 [8, 2048, 4096], P('pipe', ('seq', 'tp')), may hold values from -6 to 6
- out_grad: bfloat16 [2048, 4096], P('seq', 'tp'), may hold values from -6 to 6
- short_weights: bfloat16 [8, 7, 3, 4096], P('pipe', None, None, 'tp'), may hold values from -2 to 2
- long_filters: bfloat16 [8, 256, 128], P('pipe', 'tp'), may hold values from -0.15625 to 0.15625
- out_weights: bfloat16 [8, 4096, 4096], P('pipe', 'tp', 'seq'), may hold values from -0.09375 to 0.09375
Outputs:
- input_grad: bfloat16 [8, 2048, 4096], P('pipe', 'seq', 'tp')
- short_grad: float32 [8, 7, 3, 4096], P('pipe', None, None, 'tp')
- long_grad: float32 [8, 256, 128], P('pipe', 'tp')
All inputs are finite; a program needn't handle non-finite values.
Results may differ from a plain program's by a relative error of at most 0.03.
Values may be sent and summed in bfloat16 or wider, within the bound.
No kernel may reach another device: no remote copies, remote signals or barrier semaphores. Data moves between devices by JAX's collectives and lax.ppermute only.
A program may use at most 192 MiB of HBM per device.

v0:
```python
import jax
import jax.numpy as jnp
from jax import lax
from jax.sharding import PartitionSpec as P


def passed_along(array, axis, by):
    size = lax.axis_size(axis)
    pairs = [(i, i + by) for i in range(size) if 0 <= i + by < size]
    return lax.ppermute(array, axis, pairs)


def toeplitz_blocks(filters):
    groups, kernel_width = filters.shape
    base_row = jnp.concatenate(
        [
            jnp.zeros((groups, 1), filters.dtype),
            filters[:, ::-1],
            jnp.zeros((groups, kernel_width), filters.dtype),
        ],
        axis=1,
    )
    tiled = jnp.tile(base_row, (1, kernel_width))[:, : 2 * kernel_width * kernel_width]
    return tiled.reshape(groups, kernel_width, 2 * kernel_width)


def lag_sums(products):
    groups, kernel_width, window = products.shape
    flattened = products.reshape(groups, kernel_width * window)
    flattened = jnp.pad(flattened, ((0, 0), (0, kernel_width)))
    skewed = flattened.reshape(groups, kernel_width, window + 1)
    totals = jnp.sum(skewed, axis=1)
    return totals[:, 1 : kernel_width + 1][:, ::-1]


def to_groups(rows, groups):
    count = rows.shape[0]
    return jnp.transpose(rows.reshape(count, groups, rows.shape[1] // groups), (1, 2, 0))


def from_groups(blocks):
    groups, width, count = blocks.shape
    return jnp.transpose(blocks, (2, 0, 1)).reshape(count, groups * width)


def featurize(source, weights):
    tap_count = weights.shape[0]
    row_count = source.shape[0] - tap_count + 1
    running = jnp.zeros((weights.shape[1], row_count, source.shape[1]), jnp.float32)
    for offset in range(tap_count):
        start = tap_count - 1 - offset
        running = running + weights[offset][:, None, :] * source[start : start + row_count][None]
    return running


def spread_back(feature_grads, weights):
    tap_count = weights.shape[0]
    row_count = feature_grads.shape[1] - tap_count + 1
    running = jnp.zeros((row_count, feature_grads.shape[2]), jnp.float32)
    for offset in range(tap_count):
        running = running + jnp.sum(
            weights[offset][:, None, :] * feature_grads[:, offset : offset + row_count], axis=0
        )
    return running


def weight_grads(feature_grads, source):
    row_count = feature_grads.shape[1]
    tap_count = source.shape[0] - row_count + 1
    terms = []
    for offset in range(tap_count):
        start = tap_count - 1 - offset
        terms.append(jnp.sum(feature_grads * source[start : start + row_count][None], axis=1))
    return jnp.stack(terms)


def long_forward(padded, toeplitz, groups):
    grouped = to_groups(padded, groups)
    result = jnp.einsum("gis,gcs->gci", toeplitz, grouped, preferred_element_type=jnp.float32)
    return from_groups(result)


def long_backward(trailing, reversed_band, groups):
    grouped = to_groups(trailing, groups)
    result = jnp.einsum("grj,gcr->gcj", reversed_band, grouped, preferred_element_type=jnp.float32)
    return from_groups(result)


def filter_grads(mixed_grad, padded, groups):
    grad_groups = to_groups(mixed_grad, groups)
    value_groups = to_groups(padded, groups)
    products = jnp.einsum(
        "gci,gcs->gis", grad_groups, value_groups, preferred_element_type=jnp.float32
    )
    return lag_sums(products)


def recompute(layer_block, weights, filters):
    local_rows = lax.all_to_all(layer_block, "tp", split_axis=1, concat_axis=0, tiled=True)
    tap_count = weights.shape[0]
    kernel_width = filters.shape[1]
    before = passed_along(local_rows[local_rows.shape[0] - tap_count + 1 :], "seq", 1)
    extended = jnp.concatenate([before, local_rows], axis=0).astype(jnp.float32)
    features = featurize(extended, weights)
    products = (features[1] * features[2]).astype(jnp.bfloat16)
    earlier_products = passed_along(products[products.shape[0] - kernel_width + 1 :], "seq", 1)
    padded = jnp.concatenate(
        [jnp.zeros((1, products.shape[1]), jnp.bfloat16), earlier_products, products], axis=0
    )
    toeplitz = toeplitz_blocks(filters)
    reversed_band = jnp.concatenate(
        [toeplitz[:, :, kernel_width:], toeplitz[:, :, :kernel_width]], axis=1
    )
    mixed_rows = long_forward(padded, toeplitz, filters.shape[0])
    return (features, padded, reversed_band, mixed_rows, extended)


def dense_grad(incoming, columns, active):
    empty_sum = jnp.zeros((incoming.shape[0], columns.shape[0]), jnp.float32)
    piece = lax.all_gather(incoming, "tp", axis=1, tiled=True)
    summed = lax.cond(
        active,
        lambda: jnp.einsum("td,cd->tc", piece, columns, preferred_element_type=jnp.float32),
        lambda: empty_sum,
    )
    return summed.astype(jnp.bfloat16)


def backward(saved_state, incoming, dense_part, weights, groups, active):
    features, padded, reversed_band, mixed_rows, source = saved_state
    tap_count = weights.shape[0]
    kernel_width = reversed_band.shape[2]
    token_count, channels = incoming.shape
    edge_rows = tap_count - 1
    dense_float = dense_part.astype(jnp.float32)
    mixed_grad = (dense_float * features[0]).astype(jnp.bfloat16)
    after_grad = passed_along(mixed_grad[: kernel_width - 1], "seq", -1)
    trailing_grad = jnp.concatenate(
        [mixed_grad, after_grad, jnp.zeros((1, channels), jnp.bfloat16)], axis=0
    )

    def middle(operand):
        product_grad = long_backward(operand, reversed_band, groups)
        query_grad = dense_float * mixed_rows
        return (
            jnp.stack([query_grad, product_grad * features[2], product_grad * features[1]]),
            product_grad,
        )

    def middle_skipped(operand):
        return (
            jnp.zeros((3, token_count, channels), jnp.float32),
            jnp.zeros((token_count, channels), jnp.float32),
        )

    feature_grads, product_grad = lax.cond(active, middle, middle_skipped, trailing_grad)
    head_zeros = jnp.zeros((3, edge_rows, channels), jnp.float32)
    partial_sums = spread_back(
        jnp.concatenate([head_zeros, feature_grads[:, :edge_rows]], axis=1), weights
    )
    overflow = passed_along(partial_sums.astype(jnp.bfloat16), "seq", -1).astype(partial_sums.dtype)

    def finish(operands):
        grads, spill = operands
        trailing = jnp.concatenate([grads, head_zeros], axis=1)
        tail_rows = jnp.concatenate(
            [jnp.zeros((token_count - edge_rows, channels), jnp.float32), spill], axis=0
        )
        total = incoming.astype(jnp.float32) + spread_back(trailing, weights) + tail_rows
        return total.astype(jnp.bfloat16)

    def finish_skipped(operands):
        return jnp.zeros((token_count, channels), jnp.bfloat16)

    return (lax.cond(active, finish, finish_skipped, (feature_grads, overflow)), product_grad)


def per_device(layer_inputs, out_grad, short_weights, long_filters, out_weights):
    sections = lax.axis_size("pipe")
    section_index = lax.axis_index("pipe")
    weights = short_weights[0].astype(jnp.float32)
    filters = long_filters[0]
    groups = filters.shape[0]
    saved_state = recompute(layer_inputs[0], weights, filters)
    features, padded, reversed_band, mixed_rows, source = saved_state
    columns = lax.all_gather(out_weights[0], "seq", axis=1, tiled=True)
    incoming = out_grad
    input_result = jnp.zeros_like(out_grad)
    dense_kept = jnp.zeros(out_grad.shape, jnp.bfloat16)
    product_kept = jnp.zeros(out_grad.shape, jnp.float32)
    for step_index in range(sections):
        active = section_index == sections - 1 - step_index
        dense_part = dense_grad(incoming, columns, active)
        input_grad, product_grad = backward(
            saved_state, incoming, dense_part, weights, groups, active
        )
        input_result = jnp.where(active, input_grad, input_result)
        dense_kept = jnp.where(active, dense_part, dense_kept)
        product_kept = jnp.where(active, product_grad, product_kept)
        if step_index + 1 < sections:
            incoming = passed_along(input_grad, "pipe", -1)
    dense_float = dense_kept.astype(jnp.float32)
    mixed_grad = (dense_float * features[0]).astype(jnp.bfloat16)
    feature_grads = jnp.stack(
        [dense_float * mixed_rows, product_kept * features[2], product_kept * features[1]]
    )
    short_local = weight_grads(feature_grads, source)
    long_local = filter_grads(mixed_grad, padded, groups)
    short_result, long_result = (
        lax.psum(short_local.astype(jnp.bfloat16), "seq").astype(jnp.float32),
        lax.psum(long_local.astype(jnp.bfloat16), "seq").astype(jnp.float32),
    )
    return (input_result[None], short_result[None], long_result[None])


def solution(mesh):
    in_specs = (
        P("pipe", ("seq", "tp"), None),
        P("seq", "tp"),
        P("pipe", None, None, "tp"),
        P("pipe", "tp", None),
        P("pipe", "tp", "seq"),
    )
    out_specs = (P("pipe", "seq", "tp"), P("pipe", None, None, "tp"), P("pipe", "tp", None))
    return jax.shard_map(
        per_device, mesh=mesh, in_specs=in_specs, out_specs=out_specs, check_vma=False
    )
```

profile of v0, /device:TPU:32, one launch (start us, length us, event | category | flops | bytes accessed | tf_op | source)
XLA Modules:
  0.0 1389.2 jit_solution(17497464794075836733)
XLA Ops:
  88.4 68.1 %all-gather.27.cloned.1.call-done = bf16[1,2048,4096]{2,1,0:T(8,128)(2,1)} async-done(((bf16[1,2048,256]{2,1,0:T(8,128)(2,1)}), bf16[1,2048,4096]{2,1,0:T(8,128)(2,1)}) %all-gather.27.cloned.1.call-update) | async-done | bytes 16777232 | tf_op jit(solution)/shard_map/all_gather | solution.py:186
  235.9 56.1 %all-gather.13.cloned.1.call-done = bf16[128,4096]{1,0:T(8,128)(2,1)} async-done(((bf16[128,2048]{1,0:T(8,128)(2,1)}), bf16[128,4096]{1,0:T(8,128)(2,1)}) %all-gather.13.cloned.1.call-update) | async-done | bytes 1048592 | tf_op jit(solution)/shard_map/all_gather | solution.py:120
  298.1 14.7 %collective-permute-done.5 = bf16[127,2048]{0,1:T(8,128)(2,1)S(1)} collective-permute-done((bf16[127,2048]{0,1:T(8,128)(2,1)S(1)}, bf16[127,2048]{0,1:T(8,128)(2,1)S(1)}, u32[]{:S(2)}, u32[]{:S(2)}) %collective-permute-start.5) | collective-permute-done | bytes 520224 | tf_op jit(solution)/shard_map/ppermute | solution.py:10
  361.0 63.3 %all-gather.15.cloned.1.call-done = bf16[128,4096]{1,0:T(8,128)(2,1)} async-done(((bf16[128,2048]{1,0:T(8,128)(2,1)}), bf16[128,4096]{1,0:T(8,128)(2,1)}) %all-gather.15.cloned.1.call-update) | async-done | bytes 1048592 | tf_op jit(solution)/shard_map/all_gather | solution.py:120
  430.1 14.7 %collective-permute-done.8 = bf16[127,2048]{0,1:T(8,128)(2,1)S(1)} collective-permute-done((bf16[127,2048]{0,1:T(8,128)(2,1)S(1)}, bf16[127,2048]{0,1:T(8,128)(2,1)S(1)}, u32[]{:S(2)}, u32[]{:S(2)}) %collective-permute-start.8) | collective-permute-done | bytes 520224 | tf_op jit(solution)/shard_map/ppermute | solution.py:10
  462.6 13.9 %collective-permute-done.9 = bf16[6,2048]{0,1:T(8,128)(2,1)S(1)} collective-permute-done((bf16[6,2048]{0,1:T(8,128)(2,1)S(1)}, bf16[6,2048]{0,1:T(8,128)(2,1)S(1)}, u32[]{:S(2)}, u32[]{:S(2)}) %collective-permute-start.9) | collective-permute-done | bytes 24608 | tf_op jit(solution)/shard_map/ppermute | solution.py:10
  493.1 64.1 %all-gather.17.cloned.1.call-done = bf16[128,4096]{1,0:T(8,128)(2,1)} async-done(((bf16[128,2048]{1,0:T(8,128)(2,1)}), bf16[128,4096]{1,0:T(8,128)(2,1)}) %all-gather.17.cloned.1.call-update) | async-done | bytes 1048592 | tf_op jit(solution)/shard_map/all_gather | solution.py:120
  562.9 14.7 %collective-permute-done.11 = bf16[127,2048]{0,1:T(8,128)(2,1)S(1)} collective-permute-done((bf16[127,2048]{0,1:T(8,128)(2,1)S(1)}, bf16[127,2048]{0,1:T(8,128)(2,1)S(1)}, u32[]{:S(2)}, u32[]{:S(2)}) %collective-permute-start.11) | collective-permute-done | bytes 520224 | tf_op jit(solution)/shard_map/ppermute | solution.py:10
  595.6 13.9 %collective-permute-done.12 = bf16[6,2048]{0,1:T(8,128)(2,1)S(1)} collective-permute-done((bf16[6,2048]{0,1:T(8,128)(2,1)S(1)}, bf16[6,2048]{0,1:T(8,128)(2,1)S(1)}, u32[]{:S(2)}, u32[]{:S(2)}) %collective-permute-start.12) | collective-permute-done | bytes 24608 | tf_op jit(solution)/shard_map/ppermute | solution.py:10
  626.1 65.0 %all-gather.19.cloned.1.call-done = bf16[128,4096]{1,0:T(8,128)(2,1)} async-done(((bf16[128,2048]{1,0:T(8,128)(2,1)}), bf16[128,4096]{1,0:T(8,128)(2,1)}) %all-gather.19.cloned.1.call-update) | async-done | bytes 1048592 | tf_op jit(solution)/shard_map/all_gather | solution.py:120
  696.9 14.7 %collective-permute-done.14 = bf16[127,2048]{0,1:T(8,128)(2,1)S(1)} collective-permute-done((bf16[127,2048]{0,1:T(8,128)(2,1)S(1)}, bf16[127,2048]{0,1:T(8,128)(2,1)S(1)}, u32[]{:S(2)}, u32[]{:S(2)}) %collective-permute-start.14) | collective-permute-done | bytes 520224 | tf_op jit(solution)/shard_map/ppermute | solution.py:10
  729.2 13.9 %collective-permute-done.15 = bf16[6,2048]{0,1:T(8,128)(2,1)S(1)} collective-permute-done((bf16[6,2048]{0,1:T(8,128)(2,1)S(1)}, bf16[6,2048]{0,1:T(8,128)(2,1)S(1)}, u32[]{:S(2)}, u32[]{:S(2)}) %collective-permute-start.15) | collective-permute-done | bytes 24608 | tf_op jit(solution)/shard_map/ppermute | solution.py:10
  759.9 64.0 %all-gather.21.cloned.1.call-done = bf16[128,4096]{1,0:T(8,128)(2,1)} async-done(((bf16[128,2048]{1,0:T(8,128)(2,1)}), bf16[128,4096]{1,0:T(8,128)(2,1)}) %all-gather.21.cloned.1.call-update) | async-done | bytes 1048592 | tf_op jit(solution)/shard_map/all_gather | solution.py:120
  829.6 14.7 %collective-permute-done.17 = bf16[127,2048]{0,1:T(8,128)(2,1)S(1)} collective-permute-done((bf16[127,2048]{0,1:T(8,128)(2,1)S(1)}, bf16[127,2048]{0,1:T(8,128)(2,1)S(1)}, u32[]{:S(2)}, u32[]{:S(2)}) %collective-permute-start.17) | collective-permute-done | bytes 520224 | tf_op jit(solution)/shard_map/ppermute | solution.py:10
  880.8 57.0 %collective-permute-done.19 = bf16[128,2048]{1,0:T(8,128)(2,1)} collective-permute-done((bf16[128,2048]{1,0:T(8,128)(2,1)}, bf16[128,2048]{1,0:T(8,128)(2,1)}, u32[]{:S(2)}, u32[]{:S(2)}) %collective-permute-start.19) | collective-permute-done | bytes 524320 | tf_op jit(solution)/shard_map/ppermute | solution.py:10
  937.8 16.7 %all-gather.23.cloned.1.call-done = bf16[128,4096]{1,0:T(8,128)(2,1)} async-done(((bf16[128,2048]{1,0:T(8,128)(2,1)}), bf16[128,4096]{1,0:T(8,128)(2,1)}) %all-gather.23.cloned.1.call-update) | async-done | bytes 1048592 | tf_op jit(solution)/shard_map/all_gather | solution.py:120
  954.5 17.2 %conditional.42 = (f32[128,2048]{1,0:T(8,128)}, f32[128,2048]{0,1:T(8,128)}, bf16[128,2048]{0,1:T(8,128)(2,1)}) conditional(s32[]{:T(128)} %convert_element_type.283, () %tuple.255, (bf16[128,4096]{1,0:T(8,128)(2,1)}, bf16[2048,4096]{1,0:T(8,128)(2,1)}) %tuple.637), branch_computations={%region_115.116_spmd, %region_116.117_spmd} | conditional | flops 2148007936 | bytes 22020120 | solution.py:121
  974.4 14.7 %collective-permute-done.20 = bf16[127,2048]{0,1:T(8,128)(2,1)S(1)} collective-permute-done((bf16[127,2048]{0,1:T(8,128)(2,1)S(1)}, bf16[127,2048]{0,1:T(8,128)(2,1)S(1)}, u32[]{:S(2)}, u32[]{:S(2)}) %collective-permute-start.20) | collective-permute-done | bytes 520224 | tf_op jit(solution)/shard_map/ppermute | solution.py:10
  1017.9 13.9 %collective-permute-done.21 = bf16[6,2048]{0,1:T(8,128)(2,1)S(1)} collective-permute-done((bf16[6,2048]{0,1:T(8,128)(2,1)S(1)}, bf16[6,2048]{0,1:T(8,128)(2,1)S(1)}, u32[]{:S(2)}, u32[]{:S(2)}) %collective-permute-start.21) | collective-permute-done | bytes 24608 | tf_op jit(solution)/shard_map/ppermute | solution.py:10
  1032.9 20.9 %conditional.44 = (bf16[128,2048]{1,0:T(8,128)(2,1)}) conditional(s32[]{:T(128)} %convert_element_type.283, () %tuple.217, (bf16[128,2048]{1,0:T(8,128)(2,1)}, f32[7,3,2048]{2,1,0:T(4,128)S(1)}, f32[3,128,2048]{1,2,0:T(8,128)}, f32[6,2048]{0,1:T(8,128)}) %tuple.258), branch_computations={%region_125.126_spmd, %region_126.134_spmd} | conditional | flops 11796480 | bytes 26026020 | solution.py:175
  1099.4 17.8 %copy.274 = f32[128,128,256]{0,2,1:T(8,128)} copy(f32[128,128,256]{2,1,0:T(8,128)} %fusion.30) | data formatting | bytes 33554432 | tf_op jit(solution)/shard_map/reshape | solution.py:29
  1130.5 17.5 %reshape.203 = f32[128,128,257]{0,2,1:T(8,128)} reshape(f32[128,32896]{0,1:T(8,128)} %pad.28) | data formatting | bytes 33685504 | tf_op jit(solution)/shard_map/reshape | solution.py:31
  1158.1 77.1 %psum.15 = bf16[1,128,128]{1,2,0:T(8,128)(2,1)} all-reduce(bf16[1,128,128]{1,2,0:T(8,128)(2,1)} %bitcast.399), channel_id=1, replica_groups=mesh['pipe'=8,'seq'=16,'tp'=2] {'seq'}, use_global_device_ids=true, to_apply=%region_162.163 | all-reduce | flops 16384 | bytes 65536 | tf_op jit(solution)/shard_map/psum | solution.py:211
  1280.5 99.8 %all-reduce.27.cloned.1.call-done = bf16[1,7,3,2048]{3,1,2,0:T(8,128)(2,1)} async-done(((bf16[1,7,3,2048]{3,1,2,0:T(8,128)(2,1)}), bf16[1,7,3,2048]{3,1,2,0:T(8,128)(2,1)}) %all-reduce.27.cloned.1.call-update) | async-done | bytes 86032 | tf_op jit(solution)/shard_map/psum | solution.py:210
  (307 shorter events, 618.4 us)
Async XLA Ops:
  7.2 81.3 %all-gather.11.cloned.1.call-start = ((), (), s32[]{:S(2)}) async-start(), calls=%async_computation.1 | async-start | bytes 1572864 | tf_op jit(solution)/shard_map/all_gather | solution.py:120
  7.9 148.7 %all-gather.27.cloned.1.call-start = ((), (), s32[]{:S(2)}) async-start(), calls=%async_computation.10 | async-start | bytes 17825792 | tf_op jit(solution)/shard_map/all_gather | solution.py:186
  8.7 283.3 %all-gather.13.cloned.1.call-start = ((), (), s32[]{:S(2)}) async-start(), calls=%async_computation.2 | async-start | bytes 1572864 | tf_op jit(solution)/shard_map/all_gather | solution.py:120
  14.5 47.9 %collective-permute-start = (bf16[6,2048]{1,0:T(8,128)(2,1)S(1)}, bf16[6,2048]{1,0:T(8,128)(2,1)S(1)}, u32[]{:S(2)}, u32[]{:S(2)}) collective-permute-start(bf16[6,2048]{1,0:T(8,128)(2,1)S(1)} %slice.757), channel_id=1, source_target_pairs={{0,2},{2,4},{4,6},{6,8},{8,10},{10,12},{12,14},{14,16},{16,18},{18... | collective-permute-start | bytes 73736 | tf_op jit(solution)/shard_map/ppermute | solution.py:10
  235.8 188.6 %all-gather.15.cloned.1.call-start = ((), (), s32[]{:S(2)}) async-start(), calls=%async_computation.3 | async-start | bytes 1572864 | tf_op jit(solution)/shard_map/all_gather | solution.py:120
  296.8 16.0 %collective-permute-start.5 = (bf16[127,2048]{0,1:T(8,128)(2,1)S(1)}, bf16[127,2048]{0,1:T(8,128)(2,1)S(1)}, u32[]{:S(2)}, u32[]{:S(2)}) collective-permute-start(bf16[127,2048]{0,1:T(8,128)(2,1)S(1)} %bitcast.392), channel_id=1, source_target_pairs={{2,0},{4,2},{6,4},{8,6},{10,8},{12,10},{14,12},{16,14},{18,16},{20... | collective-permute-start | bytes 1560584 | tf_op jit(solution)/shard_map/ppermute | solution.py:10
  361.0 196.2 %all-gather.17.cloned.1.call-start = ((), (), s32[]{:S(2)}) async-start(), calls=%async_computation.4 | async-start | bytes 1572864 | tf_op jit(solution)/shard_map/all_gather | solution.py:120
  428.8 16.0 %collective-permute-start.8 = (bf16[127,2048]{0,1:T(8,128)(2,1)S(1)}, bf16[127,2048]{0,1:T(8,128)(2,1)S(1)}, u32[]{:S(2)}, u32[]{:S(2)}) collective-permute-start(bf16[127,2048]{0,1:T(8,128)(2,1)S(1)} %bitcast.393), channel_id=1, source_target_pairs={{2,0},{4,2},{6,4},{8,6},{10,8},{12,10},{14,12},{16,14},{18,16},{20... | collective-permute-start | bytes 1560584 | tf_op jit(solution)/shard_map/ppermute | solution.py:10
  461.3 15.2 %collective-permute-start.9 = (bf16[6,2048]{0,1:T(8,128)(2,1)S(1)}, bf16[6,2048]{0,1:T(8,128)(2,1)S(1)}, u32[]{:S(2)}, u32[]{:S(2)}) collective-permute-start(bf16[6,2048]{0,1:T(8,128)(2,1)S(1)} %add_convert_fusion.13), channel_id=1, source_target_pairs={{2,0},{4,2},{6,4},{8,6},{10,8},{12,10},{14,12},{16,14},{18,16},{20... | collective-permute-start | bytes 73736 | tf_op jit(solution)/shard_map/ppermute | solution.py:10
  493.0 198.1 %all-gather.19.cloned.1.call-start = ((), (), s32[]{:S(2)}) async-start(), calls=%async_computation.5 | async-start | bytes 1572864 | tf_op jit(solution)/shard_map/all_gather | solution.py:120
  561.6 16.0 %collective-permute-start.11 = (bf16[127,2048]{0,1:T(8,128)(2,1)S(1)}, bf16[127,2048]{0,1:T(8,128)(2,1)S(1)}, u32[]{:S(2)}, u32[]{:S(2)}) collective-permute-start(bf16[127,2048]{0,1:T(8,128)(2,1)S(1)} %bitcast.394), channel_id=1, source_target_pairs={{2,0},{4,2},{6,4},{8,6},{10,8},{12,10},{14,12},{16,14},{18,16},{20... | collective-permute-start | bytes 1560584 | tf_op jit(solution)/shard_map/ppermute | solution.py:10
  594.3 15.2 %collective-permute-start.12 = (bf16[6,2048]{0,1:T(8,128)(2,1)S(1)}, bf16[6,2048]{0,1:T(8,128)(2,1)S(1)}, u32[]{:S(2)}, u32[]{:S(2)}) collective-permute-start(bf16[6,2048]{0,1:T(8,128)(2,1)S(1)} %add_convert_fusion.12), channel_id=1, source_target_pairs={{2,0},{4,2},{6,4},{8,6},{10,8},{12,10},{14,12},{16,14},{18,16},{20... | collective-permute-start | bytes 73736 | tf_op jit(solution)/shard_map/ppermute | solution.py:10
  626.1 197.9 %all-gather.21.cloned.1.call-start = ((), (), s32[]{:S(2)}) async-start(), calls=%async_computation.6 | async-start | bytes 1572864 | tf_op jit(solution)/shard_map/all_gather | solution.py:120
  695.6 16.0 %collective-permute-start.14 = (bf16[127,2048]{0,1:T(8,128)(2,1)S(1)}, bf16[127,2048]{0,1:T(8,128)(2,1)S(1)}, u32[]{:S(2)}, u32[]{:S(2)}) collective-permute-start(bf16[127,2048]{0,1:T(8,128)(2,1)S(1)} %bitcast.395), channel_id=1, source_target_pairs={{2,0},{4,2},{6,4},{8,6},{10,8},{12,10},{14,12},{16,14},{18,16},{20... | collective-permute-start | bytes 1560584 | tf_op jit(solution)/shard_map/ppermute | solution.py:10
  727.9 15.2 %collective-permute-start.15 = (bf16[6,2048]{0,1:T(8,128)(2,1)S(1)}, bf16[6,2048]{0,1:T(8,128)(2,1)S(1)}, u32[]{:S(2)}, u32[]{:S(2)}) collective-permute-start(bf16[6,2048]{0,1:T(8,128)(2,1)S(1)} %add_convert_fusion.11), channel_id=1, source_target_pairs={{2,0},{4,2},{6,4},{8,6},{10,8},{12,10},{14,12},{16,14},{18,16},{20... | collective-permute-start | bytes 73736 | tf_op jit(solution)/shard_map/ppermute | solution.py:10
  759.9 194.7 %all-gather.23.cloned.1.call-start = ((), (), s32[]{:S(2)}) async-start(), calls=%async_computation.7 | async-start | bytes 1572864 | tf_op jit(solution)/shard_map/all_gather | solution.py:120
  828.3 16.0 %collective-permute-start.17 = (bf16[127,2048]{0,1:T(8,128)(2,1)S(1)}, bf16[127,2048]{0,1:T(8,128)(2,1)S(1)}, u32[]{:S(2)}, u32[]{:S(2)}) collective-permute-start(bf16[127,2048]{0,1:T(8,128)(2,1)S(1)} %bitcast.396), channel_id=1, source_target_pairs={{2,0},{4,2},{6,4},{8,6},{10,8},{12,10},{14,12},{16,14},{18,16},{20... | collective-permute-start | bytes 1560584 | tf_op jit(solution)/shard_map/ppermute | solution.py:10
  861.0 15.2 %collective-permute-start.18 = (bf16[6,2048]{0,1:T(8,128)(2,1)S(1)}, bf16[6,2048]{0,1:T(8,128)(2,1)S(1)}, u32[]{:S(2)}, u32[]{:S(2)}) collective-permute-start(bf16[6,2048]{0,1:T(8,128)(2,1)S(1)} %add_convert_fusion.10), channel_id=1, source_target_pairs={{2,0},{4,2},{6,4},{8,6},{10,8},{12,10},{14,12},{16,14},{18,16},{20... | collective-permute-start | bytes 73736 | tf_op jit(solution)/shard_map/ppermute | solution.py:10
  878.1 59.6 %collective-permute-start.19 = (bf16[128,2048]{1,0:T(8,128)(2,1)}, bf16[128,2048]{1,0:T(8,128)(2,1)}, u32[]{:S(2)}, u32[]{:S(2)}) collective-permute-start(bf16[128,2048]{1,0:T(8,128)(2,1)} %get-tuple-element.1092), channel_id=1, source_target_pairs={{32,0},{64,32},{96,64},{128,96},{160,128},{192,160},{224,192},{33,... | collective-permute-start | bytes 1572872 | tf_op jit(solution)/shard_map/ppermute | solution.py:10
  937.8 146.2 %all-gather.25.cloned.1.call-start = ((), (), s32[]{:S(2)}) async-start(), calls=%async_computation.8 | async-start | bytes 1572864 | tf_op jit(solution)/shard_map/all_gather | solution.py:120
  973.1 16.0 %collective-permute-start.20 = (bf16[127,2048]{0,1:T(8,128)(2,1)S(1)}, bf16[127,2048]{0,1:T(8,128)(2,1)S(1)}, u32[]{:S(2)}, u32[]{:S(2)}) collective-permute-start(bf16[127,2048]{0,1:T(8,128)(2,1)S(1)} %bitcast.397), channel_id=1, source_target_pairs={{2,0},{4,2},{6,4},{8,6},{10,8},{12,10},{14,12},{16,14},{18,16},{20... | collective-permute-start | bytes 1560584 | tf_op jit(solution)/shard_map/ppermute | solution.py:10
  1016.6 15.2 %collective-permute-start.21 = (bf16[6,2048]{0,1:T(8,128)(2,1)S(1)}, bf16[6,2048]{0,1:T(8,128)(2,1)S(1)}, u32[]{:S(2)}, u32[]{:S(2)}) collective-permute-start(bf16[6,2048]{0,1:T(8,128)(2,1)S(1)} %add_convert_fusion.9), channel_id=1, source_target_pairs={{2,0},{4,2},{6,4},{8,6},{10,8},{12,10},{14,12},{16,14},{18,16},{20... | collective-permute-start | bytes 73736 | tf_op jit(solution)/shard_map/ppermute | solution.py:10
  1068.4 311.9 %all-reduce.27.cloned.1.call-start = ((), (), s32[]{:S(2)}) async-start(), calls=%async_computation.9 | async-start | bytes 196608 | tf_op jit(solution)/shard_map/psum | solution.py:210
  1090.0 149.2 %collective-permute-start.23 = (bf16[127,2048]{0,1:T(8,128)(2,1)}, bf16[127,2048]{0,1:T(8,128)(2,1)}, u32[]{:S(2)}, u32[]{:S(2)}) collective-permute-start(bf16[127,2048]{0,1:T(8,128)(2,1)} %bitcast.351), channel_id=1, source_target_pairs={{2,0},{4,2},{6,4},{8,6},{10,8},{12,10},{14,12},{16,14},{18,16},{20... | collective-permute-start | bytes 1560584 | tf_op jit(solution)/shard_map/ppermute | solution.py:10
  (41 other events, 276.8 us)
Sparse Core Ops, SparseCore 0:
  9.8 16.9 all-gather.10
  29.2 127.3 all-gather.26
  235.9 55.9 all-gather.12
  361.1 63.2 all-gather.14
  493.1 63.9 all-gather.16
  626.2 64.8 all-gather.18
  760.0 63.8 all-gather.20
  937.9 16.6 all-gather.22
  1068.5 15.4 all-gather.24
  1268.5 111.7 all-reduce.26
where the time goes:
time: 1400 us; the launch traced here: 1390 us
  waiting for transfers between devices  826 us (59%)
  local copies, waits for them, and re-layouts  195 us (14%)
  other arithmetic  189 us (14%)
  blocking collectives  81.3 us (6%)
  starting transfers between devices  45.8 us (3%)
  matrix products  32.7 us (2%)
  between operations  15.6 us (1%)
    all_gather x8, waiting for transfers between devices, dense_grad(): piece = lax.all_gather(incoming, 'tp', axis=1, tiled=True)  330 us
    ppermute x25, waiting for transfers between devices, passed_along(): return lax.ppermute(array, axis, pairs)  327 us
    psum x1, waiting for transfers between devices, per_device(): lax.psum(short_local.astype(jnp.bfloat16), 'seq').astype(jnp.float32)  99.8 us
    reduce_sum x10, other arithmetic, spread_back(): jnp.sum(weights[offset][:, None, :] * feature_grads[:, offset:offset + ro...  88.6 us
    psum x1, blocking collectives, per_device(): lax.psum(long_local.astype(jnp.bfloat16), 'seq').astype(jnp.float32)  77.1 us
    all_gather x1, waiting for transfers between devices, per_device(): columns = lax.all_gather(out_weights[0], 'seq', axis=1, tiled=True)  68.1 us
    another operation x46, local copies, waits for them, and re-layouts  50.6 us
    ppermute x25, starting transfers between devices, passed_along(): return lax.ppermute(array, axis, pairs)  45.4 us
  transfers between devices with their start and end apart: 35, of which 32 were waited for; matrix products, arithmetic and copies ran while one was open for 12% of the time, Pallas kernels for 0%

commit v1 on v0

--- a/solution.py
+++ b/solution.py
@@ -207,7 +207,9 @@
     short_local = weight_grads(feature_grads, source)
     long_local = filter_grads(mixed_grad, padded, groups)
     short_result, long_result = (
-        lax.psum(short_local.astype(jnp.bfloat16), "seq").astype(jnp.float32),
+        jnp.sum(lax.all_gather(short_local.astype(jnp.bfloat16), "seq"), axis=0).astype(
+            jnp.float32
+        ),
         lax.psum(long_local.astype(jnp.bfloat16), "seq").astype(jnp.float32),
     )
     return (input_result[None], short_result[None], long_result[None])

time: 1400 us -> 1340 us (0.957)
  the two profiles are of different devices: /device:TPU:32 before, /device:TPU:0 now
where the time goes in v1:
time: 1340 us; the launch traced here: 1330 us
  waiting for transfers between devices  791 us (59%)
  local copies, waits for them, and re-layouts  189 us (14%)
  other arithmetic  184 us (14%)
  blocking collectives  80.9 us (6%)
  starting transfers between devices  35.7 us (3%)
  matrix products  33.6 us (3%)
  between operations  15.7 us (1%)
    all_gather x8, waiting for transfers between devices, dense_grad(): piece = lax.all_gather(incoming, 'tp', axis=1, tiled=True)  395 us
    ppermute x25, waiting for transfers between devices, passed_along(): return lax.ppermute(array, axis, pairs)  327 us
    reduce_sum x10, other arithmetic, spread_back(): jnp.sum(weights[offset][:, None, :] * feature_grads[:, offset:offset + ro...  82 us
    psum x1, blocking collectives, per_device(): lax.psum(long_local.astype(jnp.bfloat16), 'seq').astype(jnp.float32)  76.7 us
    all_gather x1, waiting for transfers between devices, per_device(): columns = lax.all_gather(out_weights[0], 'seq', axis=1, tiled=True)  68 us
    another operation x46, local copies, waits for them, and re-layouts  46.8 us
    ppermute x25, starting transfers between devices, passed_along(): return lax.ppermute(array, axis, pairs)  35.3 us
  transfers between devices with their start and end apart: 35, of which 30 were waited for; matrix products, arithmetic and copies ran while one was open for 14% of the time, Pallas kernels for 0%

profile of v1, /device:TPU:0, one launch (start us, length us, event | category | flops | bytes accessed | tf_op | source)
XLA Modules:
  0.0 1332.4 jit_solution(16699903494795010281)
XLA Ops:
  87.2 68.0 %all-gather.30.cloned.1.call-done = bf16[1,2048,4096]{2,1,0:T(8,128)(2,1)} async-done(((bf16[1,2048,256]{2,1,0:T(8,128)(2,1)}), bf16[1,2048,4096]{2,1,0:T(8,128)(2,1)}) %all-gather.30.cloned.1.call-update) | async-done | bytes 16777232 | tf_op jit(solution)/shard_map/all_gather | solution.py:186
  234.5 56.9 %all-gather.14.cloned.1.call-done = bf16[128,4096]{1,0:T(8,128)(2,1)} async-done(((bf16[128,2048]{1,0:T(8,128)(2,1)}), bf16[128,4096]{1,0:T(8,128)(2,1)}) %all-gather.14.cloned.1.call-update) | async-done | bytes 1048592 | tf_op jit(solution)/shard_map/all_gather | solution.py:120
  297.5 14.7 %collective-permute-done.5 = bf16[127,2048]{0,1:T(8,128)(2,1)S(1)} collective-permute-done((bf16[127,2048]{0,1:T(8,128)(2,1)S(1)}, bf16[127,2048]{0,1:T(8,128)(2,1)S(1)}, u32[]{:S(2)}, u32[]{:S(2)}) %collective-permute-start.5) | collective-permute-done | bytes 520224 | tf_op jit(solution)/shard_map/ppermute | solution.py:10
  329.8 13.9 %collective-permute-done.6 = bf16[6,2048]{0,1:T(8,128)(2,1)S(1)} collective-permute-done((bf16[6,2048]{0,1:T(8,128)(2,1)S(1)}, bf16[6,2048]{0,1:T(8,128)(2,1)S(1)}, u32[]{:S(2)}, u32[]{:S(2)}) %collective-permute-start.6) | collective-permute-done | bytes 24608 | tf_op jit(solution)/shard_map/ppermute | solution.py:10
  360.5 64.0 %all-gather.16.cloned.1.call-done = bf16[128,4096]{1,0:T(8,128)(2,1)} async-done(((bf16[128,2048]{1,0:T(8,128)(2,1)}), bf16[128,4096]{1,0:T(8,128)(2,1)}) %all-gather.16.cloned.1.call-update) | async-done | bytes 1048592 | tf_op jit(solution)/shard_map/all_gather | solution.py:120
  430.3 14.7 %collective-permute-done.8 = bf16[127,2048]{0,1:T(8,128)(2,1)S(1)} collective-permute-done((bf16[127,2048]{0,1:T(8,128)(2,1)S(1)}, bf16[127,2048]{0,1:T(8,128)(2,1)S(1)}, u32[]{:S(2)}, u32[]{:S(2)}) %collective-permute-start.8) | collective-permute-done | bytes 520224 | tf_op jit(solution)/shard_map/ppermute | solution.py:10
  462.8 13.9 %collective-permute-done.9 = bf16[6,2048]{0,1:T(8,128)(2,1)S(1)} collective-permute-done((bf16[6,2048]{0,1:T(8,128)(2,1)S(1)}, bf16[6,2048]{0,1:T(8,128)(2,1)S(1)}, u32[]{:S(2)}, u32[]{:S(2)}) %collective-permute-start.9) | collective-permute-done | bytes 24608 | tf_op jit(solution)/shard_map/ppermute | solution.py:10
  493.3 64.9 %all-gather.18.cloned.1.call-done = bf16[128,4096]{1,0:T(8,128)(2,1)} async-done(((bf16[128,2048]{1,0:T(8,128)(2,1)}), bf16[128,4096]{1,0:T(8,128)(2,1)}) %all-gather.18.cloned.1.call-update) | async-done | bytes 1048592 | tf_op jit(solution)/shard_map/all_gather | solution.py:120
  563.8 14.7 %collective-permute-done.11 = bf16[127,2048]{0,1:T(8,128)(2,1)S(1)} collective-permute-done((bf16[127,2048]{0,1:T(8,128)(2,1)S(1)}, bf16[127,2048]{0,1:T(8,128)(2,1)S(1)}, u32[]{:S(2)}, u32[]{:S(2)}) %collective-permute-start.11) | collective-permute-done | bytes 520224 | tf_op jit(solution)/shard_map/ppermute | solution.py:10
  627.1 65.7 %all-gather.20.cloned.1.call-done = bf16[128,4096]{1,0:T(8,128)(2,1)} async-done(((bf16[128,2048]{1,0:T(8,128)(2,1)}), bf16[128,4096]{1,0:T(8,128)(2,1)}) %all-gather.20.cloned.1.call-update) | async-done | bytes 1048592 | tf_op jit(solution)/shard_map/all_gather | solution.py:120
  698.5 14.7 %collective-permute-done.14 = bf16[127,2048]{0,1:T(8,128)(2,1)S(1)} collective-permute-done((bf16[127,2048]{0,1:T(8,128)(2,1)S(1)}, bf16[127,2048]{0,1:T(8,128)(2,1)S(1)}, u32[]{:S(2)}, u32[]{:S(2)}) %collective-permute-start.14) | collective-permute-done | bytes 520224 | tf_op jit(solution)/shard_map/ppermute | solution.py:10
  730.9 13.9 %collective-permute-done.15 = bf16[6,2048]{0,1:T(8,128)(2,1)S(1)} collective-permute-done((bf16[6,2048]{0,1:T(8,128)(2,1)S(1)}, bf16[6,2048]{0,1:T(8,128)(2,1)S(1)}, u32[]{:S(2)}, u32[]{:S(2)}) %collective-permute-start.15) | collective-permute-done | bytes 24608 | tf_op jit(solution)/shard_map/ppermute | solution.py:10
  761.6 64.6 %all-gather.22.cloned.1.call-done = bf16[128,4096]{1,0:T(8,128)(2,1)} async-done(((bf16[128,2048]{1,0:T(8,128)(2,1)}), bf16[128,4096]{1,0:T(8,128)(2,1)}) %all-gather.22.cloned.1.call-update) | async-done | bytes 1048592 | tf_op jit(solution)/shard_map/all_gather | solution.py:120
  831.9 14.7 %collective-permute-done.17 = bf16[127,2048]{0,1:T(8,128)(2,1)S(1)} collective-permute-done((bf16[127,2048]{0,1:T(8,128)(2,1)S(1)}, bf16[127,2048]{0,1:T(8,128)(2,1)S(1)}, u32[]{:S(2)}, u32[]{:S(2)}) %collective-permute-start.17) | collective-permute-done | bytes 520224 | tf_op jit(solution)/shard_map/ppermute | solution.py:10
  864.6 13.9 %collective-permute-done.18 = bf16[6,2048]{0,1:T(8,128)(2,1)S(1)} collective-permute-done((bf16[6,2048]{0,1:T(8,128)(2,1)S(1)}, bf16[6,2048]{0,1:T(8,128)(2,1)S(1)}, u32[]{:S(2)}, u32[]{:S(2)}) %collective-permute-start.18) | collective-permute-done | bytes 24608 | tf_op jit(solution)/shard_map/ppermute | solution.py:10
  895.1 62.5 %all-gather.24.cloned.1.call-done = bf16[128,4096]{1,0:T(8,128)(2,1)} async-done(((bf16[128,2048]{1,0:T(8,128)(2,1)}), bf16[128,4096]{1,0:T(8,128)(2,1)}) %all-gather.24.cloned.1.call-update) | async-done | bytes 1048592 | tf_op jit(solution)/shard_map/all_gather | solution.py:120
  963.2 14.7 %collective-permute-done.20 = bf16[127,2048]{0,1:T(8,128)(2,1)S(1)} collective-permute-done((bf16[127,2048]{0,1:T(8,128)(2,1)S(1)}, bf16[127,2048]{0,1:T(8,128)(2,1)S(1)}, u32[]{:S(2)}, u32[]{:S(2)}) %collective-permute-start.20) | collective-permute-done | bytes 520224 | tf_op jit(solution)/shard_map/ppermute | solution.py:10
  1012.8 58.8 %collective-permute-done.22 = bf16[128,2048]{1,0:T(8,128)(2,1)} collective-permute-done((bf16[128,2048]{1,0:T(8,128)(2,1)}, bf16[128,2048]{1,0:T(8,128)(2,1)}, u32[]{:S(2)}, u32[]{:S(2)}) %collective-permute-start.22) | collective-permute-done | bytes 524320 | tf_op jit(solution)/shard_map/ppermute | solution.py:10
  1071.7 16.0 %all-gather.26.cloned.1.call-done = bf16[128,4096]{1,0:T(8,128)(2,1)} async-done(((bf16[128,2048]{1,0:T(8,128)(2,1)}), bf16[128,4096]{1,0:T(8,128)(2,1)}) %all-gather.26.cloned.1.call-update) | async-done | bytes 1048592 | tf_op jit(solution)/shard_map/all_gather | solution.py:120
  1087.7 17.5 %conditional.45 = (f32[128,2048]{1,0:T(8,128)}, f32[128,2048]{0,1:T(8,128)}, bf16[128,2048]{0,1:T(8,128)(2,1)}) conditional(s32[]{:T(128)} %convert_element_type.303, () %tuple.260, (bf16[128,4096]{1,0:T(8,128)(2,1)}, bf16[2048,4096]{1,0:T(8,128)(2,1)}) %tuple.655), branch_computations={%region_134.135_spmd, %region_135.136_spmd} | conditional | flops 2148007936 | bytes 22020120 | solution.py:121
  1127.8 15.1 %conditional.46 = (f32[3,128,2048]{1,2,0:T(8,128)}, f32[128,2048]{0,1:T(8,128)}) conditional(s32[]{:T(128)} %convert_element_type.303, () %tuple.259, (f32[128,2048]{1,0:T(8,128)}, f32[128,2048]{0,1:T(8,128)}, bf16[256,2048]{0,1:T(8,128)(2,1)S(1)}, bf16[128,256,128]{2,1,0:T(8,128)(2,1)}, f32[3,128,2048]{1,2,0:T(8,128)S(1)}) %tuple.663), branch_computations={%region_136.137_spmd, %region_137.138_spmd} | conditional | flops 136577024 | bytes 35651656 | solution.py:156
  1175.5 17.8 %copy.335 = f32[128,128,256]{0,2,1:T(8,128)} copy(f32[128,128,256]{2,1,0:T(8,128)} %fusion.30) | data formatting | bytes 33554432 | tf_op jit(solution)/shard_map/reshape | solution.py:29
  1206.7 17.5 %reshape.320 = f32[128,128,257]{0,2,1:T(8,128)} reshape(f32[128,32896]{0,1:T(8,128)} %pad.28) | data formatting | bytes 33685504 | tf_op jit(solution)/shard_map/reshape | solution.py:31
  1231.0 76.7 %psum.7 = bf16[1,128,128]{1,2,0:T(8,128)(2,1)S(1)} all-reduce(bf16[1,128,128]{1,2,0:T(8,128)(2,1)S(1)} %bitcast.398), channel_id=1, replica_groups=mesh['pipe'=8,'seq'=16,'tp'=2] {'seq'}, use_global_device_ids=true, to_apply=%region_162.163 | all-reduce | flops 16384 | bytes 65536 | tf_op jit(solution)/shard_map/psum | solution.py:213
  (312 shorter events, 591.8 us)
Async XLA Ops:
  7.2 80.0 %all-gather.12.cloned.1.call-start = ((), (), s32[]{:S(2)}) async-start(), calls=%async_computation.1 | async-start | bytes 1572864 | tf_op jit(solution)/shard_map/all_gather | solution.py:120
  7.9 147.3 %all-gather.30.cloned.1.call-start = ((), (), s32[]{:S(2)}) async-start(), calls=%async_computation.10 | async-start | bytes 17825792 | tf_op jit(solution)/shard_map/all_gather | solution.py:186
  8.7 282.8 %all-gather.14.cloned.1.call-start = ((), (), s32[]{:S(2)}) async-start(), calls=%async_computation.2 | async-start | bytes 1572864 | tf_op jit(solution)/shard_map/all_gather | solution.py:120
  14.5 46.4 %collective-permute-start = (bf16[6,2048]{1,0:T(8,128)(2,1)S(1)}, bf16[6,2048]{1,0:T(8,128)(2,1)S(1)}, u32[]{:S(2)}, u32[]{:S(2)}) collective-permute-start(bf16[6,2048]{1,0:T(8,128)(2,1)S(1)} %slice.757), channel_id=1, source_target_pairs={{0,2},{2,4},{4,6},{6,8},{8,10},{10,12},{12,14},{14,16},{16,18},{18... | collective-permute-start | bytes 73736 | tf_op jit(solution)/shard_map/ppermute | solution.py:10
  234.5 190.1 %all-gather.16.cloned.1.call-start = ((), (), s32[]{:S(2)}) async-start(), calls=%async_computation.3 | async-start | bytes 1572864 | tf_op jit(solution)/shard_map/all_gather | solution.py:120
  296.2 16.0 %collective-permute-start.5 = (bf16[127,2048]{0,1:T(8,128)(2,1)S(1)}, bf16[127,2048]{0,1:T(8,128)(2,1)S(1)}, u32[]{:S(2)}, u32[]{:S(2)}) collective-permute-start(bf16[127,2048]{0,1:T(8,128)(2,1)S(1)} %bitcast.392), channel_id=1, source_target_pairs={{2,0},{4,2},{6,4},{8,6},{10,8},{12,10},{14,12},{16,14},{18,16},{20... | collective-permute-start | bytes 1560584 | tf_op jit(solution)/shard_map/ppermute | solution.py:10
  328.5 15.2 %collective-permute-start.6 = (bf16[6,2048]{0,1:T(8,128)(2,1)S(1)}, bf16[6,2048]{0,1:T(8,128)(2,1)S(1)}, u32[]{:S(2)}, u32[]{:S(2)}) collective-permute-start(bf16[6,2048]{0,1:T(8,128)(2,1)S(1)} %add_convert_fusion.14), channel_id=1, source_target_pairs={{2,0},{4,2},{6,4},{8,6},{10,8},{12,10},{14,12},{16,14},{18,16},{20... | collective-permute-start | bytes 73736 | tf_op jit(solution)/shard_map/ppermute | solution.py:10
  360.5 197.7 %all-gather.18.cloned.1.call-start = ((), (), s32[]{:S(2)}) async-start(), calls=%async_computation.4 | async-start | bytes 1572864 | tf_op jit(solution)/shard_map/all_gather | solution.py:120
  429.0 16.0 %collective-permute-start.8 = (bf16[127,2048]{0,1:T(8,128)(2,1)S(1)}, bf16[127,2048]{0,1:T(8,128)(2,1)S(1)}, u32[]{:S(2)}, u32[]{:S(2)}) collective-permute-start(bf16[127,2048]{0,1:T(8,128)(2,1)S(1)} %bitcast.393), channel_id=1, source_target_pairs={{2,0},{4,2},{6,4},{8,6},{10,8},{12,10},{14,12},{16,14},{18,16},{20... | collective-permute-start | bytes 1560584 | tf_op jit(solution)/shard_map/ppermute | solution.py:10
  461.5 15.2 %collective-permute-start.9 = (bf16[6,2048]{0,1:T(8,128)(2,1)S(1)}, bf16[6,2048]{0,1:T(8,128)(2,1)S(1)}, u32[]{:S(2)}, u32[]{:S(2)}) collective-permute-start(bf16[6,2048]{0,1:T(8,128)(2,1)S(1)} %add_convert_fusion.13), channel_id=1, source_target_pairs={{2,0},{4,2},{6,4},{8,6},{10,8},{12,10},{14,12},{16,14},{18,16},{20... | collective-permute-start | bytes 73736 | tf_op jit(solution)/shard_map/ppermute | solution.py:10
  493.2 199.5 %all-gather.20.cloned.1.call-start = ((), (), s32[]{:S(2)}) async-start(), calls=%async_computation.5 | async-start | bytes 1572864 | tf_op jit(solution)/shard_map/all_gather | solution.py:120
  562.5 16.0 %collective-permute-start.11 = (bf16[127,2048]{0,1:T(8,128)(2,1)S(1)}, bf16[127,2048]{0,1:T(8,128)(2,1)S(1)}, u32[]{:S(2)}, u32[]{:S(2)}) collective-permute-start(bf16[127,2048]{0,1:T(8,128)(2,1)S(1)} %bitcast.394), channel_id=1, source_target_pairs={{2,0},{4,2},{6,4},{8,6},{10,8},{12,10},{14,12},{16,14},{18,16},{20... | collective-permute-start | bytes 1560584 | tf_op jit(solution)/shard_map/ppermute | solution.py:10
  627.0 199.2 %all-gather.22.cloned.1.call-start = ((), (), s32[]{:S(2)}) async-start(), calls=%async_computation.6 | async-start | bytes 1572864 | tf_op jit(solution)/shard_map/all_gather | solution.py:120
  697.2 16.0 %collective-permute-start.14 = (bf16[127,2048]{0,1:T(8,128)(2,1)S(1)}, bf16[127,2048]{0,1:T(8,128)(2,1)S(1)}, u32[]{:S(2)}, u32[]{:S(2)}) collective-permute-start(bf16[127,2048]{0,1:T(8,128)(2,1)S(1)} %bitcast.395), channel_id=1, source_target_pairs={{2,0},{4,2},{6,4},{8,6},{10,8},{12,10},{14,12},{16,14},{18,16},{20... | collective-permute-start | bytes 1560584 | tf_op jit(solution)/shard_map/ppermute | solution.py:10
  729.6 15.2 %collective-permute-start.15 = (bf16[6,2048]{0,1:T(8,128)(2,1)S(1)}, bf16[6,2048]{0,1:T(8,128)(2,1)S(1)}, u32[]{:S(2)}, u32[]{:S(2)}) collective-permute-start(bf16[6,2048]{0,1:T(8,128)(2,1)S(1)} %add_convert_fusion.11), channel_id=1, source_target_pairs={{2,0},{4,2},{6,4},{8,6},{10,8},{12,10},{14,12},{16,14},{18,16},{20... | collective-permute-start | bytes 73736 | tf_op jit(solution)/shard_map/ppermute | solution.py:10
  761.5 196.0 %all-gather.24.cloned.1.call-start = ((), (), s32[]{:S(2)}) async-start(), calls=%async_computation.7 | async-start | bytes 1572864 | tf_op jit(solution)/shard_map/all_gather | solution.py:120
  830.6 16.0 %collective-permute-start.17 = (bf16[127,2048]{0,1:T(8,128)(2,1)S(1)}, bf16[127,2048]{0,1:T(8,128)(2,1)S(1)}, u32[]{:S(2)}, u32[]{:S(2)}) collective-permute-start(bf16[127,2048]{0,1:T(8,128)(2,1)S(1)} %bitcast.396), channel_id=1, source_target_pairs={{2,0},{4,2},{6,4},{8,6},{10,8},{12,10},{14,12},{16,14},{18,16},{20... | collective-permute-start | bytes 1560584 | tf_op jit(solution)/shard_map/ppermute | solution.py:10
  863.3 15.2 %collective-permute-start.18 = (bf16[6,2048]{0,1:T(8,128)(2,1)S(1)}, bf16[6,2048]{0,1:T(8,128)(2,1)S(1)}, u32[]{:S(2)}, u32[]{:S(2)}) collective-permute-start(bf16[6,2048]{0,1:T(8,128)(2,1)S(1)} %add_convert_fusion.10), channel_id=1, source_target_pairs={{2,0},{4,2},{6,4},{8,6},{10,8},{12,10},{14,12},{16,14},{18,16},{20... | collective-permute-start | bytes 73736 | tf_op jit(solution)/shard_map/ppermute | solution.py:10
  895.0 192.6 %all-gather.26.cloned.1.call-start = ((), (), s32[]{:S(2)}) async-start(), calls=%async_computation.8 | async-start | bytes 1572864 | tf_op jit(solution)/shard_map/all_gather | solution.py:120
  961.9 16.0 %collective-permute-start.20 = (bf16[127,2048]{0,1:T(8,128)(2,1)S(1)}, bf16[127,2048]{0,1:T(8,128)(2,1)S(1)}, u32[]{:S(2)}, u32[]{:S(2)}) collective-permute-start(bf16[127,2048]{0,1:T(8,128)(2,1)S(1)} %bitcast.397), channel_id=1, source_target_pairs={{2,0},{4,2},{6,4},{8,6},{10,8},{12,10},{14,12},{16,14},{18,16},{20... | collective-permute-start | bytes 1560584 | tf_op jit(solution)/shard_map/ppermute | solution.py:10
  1011.5 60.1 %collective-permute-start.22 = (bf16[128,2048]{1,0:T(8,128)(2,1)}, bf16[128,2048]{1,0:T(8,128)(2,1)}, u32[]{:S(2)}, u32[]{:S(2)}) collective-permute-start(bf16[128,2048]{1,0:T(8,128)(2,1)} %get-tuple-element.1168), channel_id=1, source_target_pairs={{32,0},{64,32},{96,64},{128,96},{160,128},{192,160},{224,192},{33,... | collective-permute-start | bytes 1572872 | tf_op jit(solution)/shard_map/ppermute | solution.py:10
  1071.6 250.9 %all-gather.28.cloned.1.call-start = ((), (), s32[]{:S(2)}) async-start(), calls=%async_computation.9 | async-start | bytes 1671168 | tf_op jit(solution)/shard_map/all_gather | solution.py:210
  1107.9 18.2 %collective-permute-start.23 = (bf16[127,2048]{0,1:T(8,128)(2,1)}, bf16[127,2048]{0,1:T(8,128)(2,1)}, u32[]{:S(2)}, u32[]{:S(2)}) collective-permute-start(bf16[127,2048]{0,1:T(8,128)(2,1)} %bitcast.351), channel_id=1, source_target_pairs={{2,0},{4,2},{6,4},{8,6},{10,8},{12,10},{14,12},{16,14},{18,16},{20... | collective-permute-start | bytes 1560584 | tf_op jit(solution)/shard_map/ppermute | solution.py:10
  1166.0 142.4 %collective-permute-start.24 = (bf16[6,2048]{0,1:T(8,128)(2,1)S(1)}, bf16[6,2048]{0,1:T(8,128)(2,1)S(1)}, u32[]{:S(2)}, u32[]{:S(2)}) collective-permute-start(bf16[6,2048]{0,1:T(8,128)(2,1)S(1)} %add_convert_fusion.8), channel_id=1, source_target_pairs={{2,0},{4,2},{6,4},{8,6},{10,8},{12,10},{14,12},{16,14},{18,16},{20... | collective-permute-start | bytes 73736 | tf_op jit(solution)/shard_map/ppermute | solution.py:10
  (42 other events, 267.3 us)
Sparse Core Ops, SparseCore 0:
  9.8 15.8 all-gather.11
  28.1 127.0 all-gather.29
  234.6 56.8 all-gather.13
  360.6 63.8 all-gather.15
  493.4 64.7 all-gather.17
  627.1 65.5 all-gather.19
  761.6 64.5 all-gather.21
  895.1 62.3 all-gather.23
  1071.7 15.8 all-gather.25
  1153.8 50.0 all-gather.27
